TPU v7x, 32 devices: a whole 2x2x4 slice. The times are simulated.
32 devices in a mesh: region: 4 (over y, x), block: 8 (over z, core).
Axes of the slice: x: 2, y: 2, z: 4, core: 2. Of those that a mesh axis runs over, the one named last changes fastest.
Arguments:
- obs: bfloat16 [512, 32, 128], P(('region', 'block')), may hold values from -6 to 6
- predict: bfloat16 [512, 2, 128, 128], P(('region', 'block')), may hold values from -0.375 to 0.375
- factor: bfloat16 [512, 128, 128], P(('region', 'block')), as said below
- tau: float32 [32], replicated, may hold values from 0.5 to 2
- nbr_dev: int32 [512, 1], P(('region', 'block')), may hold values from 0 to 7; in each aligned block of 16 rows (0 to 15, 16 to 31, ...) at most 4 rows name the same one
- nbr_slot: int32 [512, 2], P(('region', 'block')), may hold values from 0 to 15
- counts: int32 [32], P(('region', 'block')), may hold values from 8 to 16
Outputs:
- grad_obs: float32 [512, 32, 128], P(('region', 'block'))
- grad_tau: float32 [32], replicated
Inputs may be any that keep to these rules, and one draw needn't show every extreme that they name: `nbr_dev`: among the blocks of one device at most 4 name the same device. `nbr_slot`: column 0 is a slot on the in-region neighbour's device, column 1 a slot on the device of the previous region with the same index along block. `factor`: each block's matrix is the identity plus small entries.
All inputs are finite; a program needn't handle non-finite values.
Results may differ from a plain program's by a relative error of at most 0.0035.
Values may be sent and summed in bfloat16 or wider, within the bound.
A program may use at most 64 MiB of HBM per device.

v0:
```python
import jax
import jax.numpy as jnp
from jax import lax
from jax.sharding import PartitionSpec as P


def passed_along(value, axis, steps):
    count = lax.axis_size(axis)
    leading, last = (max(0, -steps), min(count, count - steps))
    return lax.ppermute(value, axis, [(source, source + steps) for source in range(leading, last)])


def shards(obs, predict, factor, tau, nbr_dev, nbr_slot, counts):
    nbd = obs.shape[0]
    chans = obs.shape[1]
    width = obs.shape[2]
    nblock = lax.axis_size("block")
    cap_size = max(2, 2 * nbd // nblock)
    total_slots = nblock * cap_size
    dest = nbr_dev[:, 0]
    slot_one = nbr_slot[:, 0]
    slot_two = nbr_slot[:, 1]
    onehot = (dest[:, None] == jnp.arange(nblock, dtype=jnp.int32)[None, :]).astype(jnp.int32)
    before = jnp.cumsum(onehot, axis=0) - onehot
    rank_in = jnp.sum(before * onehot, axis=1)
    flat = dest * cap_size + rank_in
    match = (flat[:, None] == jnp.arange(total_slots, dtype=jnp.int32)[None, :]).astype(jnp.int32)
    filled = jnp.sum(match, axis=0)
    req_flat = jnp.sum(match * slot_one[:, None], axis=0) + (1 - filled) * nbd
    request = req_flat.reshape(nblock, cap_size)
    region_all = lax.all_gather(obs, "block", axis=0, tiled=True)
    near = jnp.take(region_all, dest * nbd + slot_one, axis=0)
    previous = passed_along(obs, "region", 1)
    far = jnp.take(previous, slot_two, axis=0)
    p_zero = predict[:, 0]
    p_one = predict[:, 1]
    err = obs.astype(jnp.float32) - jnp.einsum(
        "bcj,bjk->bck", near, p_zero, preferred_element_type=jnp.float32
    )
    err = err - jnp.einsum("bcj,bjk->bck", far, p_one, preferred_element_type=jnp.float32)
    err = err.astype(jnp.bfloat16)
    white = jnp.einsum("bcj,bjk->bck", err, factor, preferred_element_type=jnp.float32)
    live = (jnp.arange(nbd, dtype=jnp.int32) < counts[0]).astype(jnp.float32)
    weighted = (live[:, None, None] * tau[None, :, None] * white).astype(jnp.bfloat16)
    adj = jnp.einsum("bck,bjk->bcj", weighted, factor, preferred_element_type=jnp.float32)
    adj16 = adj.astype(jnp.bfloat16)
    back_one = -jnp.einsum("bck,bjk->bcj", adj16, p_zero, preferred_element_type=jnp.float32)
    back_two = -jnp.einsum("bck,bjk->bcj", adj16, p_one, preferred_element_type=jnp.float32)
    placed = jnp.einsum(
        "bs,bcj->scj", match.astype(jnp.float32), back_one, precision=lax.Precision.HIGHEST
    )
    placed = placed.reshape(nblock, cap_size, chans, width)
    returned, owned_slots = (
        lax.all_to_all(placed, "block", split_axis=0, concat_axis=0, tiled=True),
        lax.all_to_all(request, "block", split_axis=0, concat_axis=0, tiled=True),
    )
    spread = (owned_slots.reshape(-1)[:, None] == jnp.arange(nbd, dtype=jnp.int32)[None, :]).astype(
        jnp.float32
    )
    add_one = jnp.einsum(
        "sb,scj->bcj",
        spread,
        returned.reshape(total_slots, chans, width),
        precision=lax.Precision.HIGHEST,
    )
    seam_hot = (slot_two[:, None] == jnp.arange(nbd, dtype=jnp.int32)[None, :]).astype(jnp.float32)
    seam_dense = jnp.einsum("bs,bcj->scj", seam_hot, back_two, precision=lax.Precision.HIGHEST)
    add_two = passed_along(seam_dense, "region", -1)
    grad_obs = adj + add_one + add_two
    squares = jnp.sum(live[:, None, None] * white * white, axis=(0, 2))
    live_count = jnp.sum(live)
    total_sq, total_live = lax.psum((squares, live_count), ("region", "block"))
    all_blocks = nbd * lax.axis_size("region") * nblock
    grad_tau = (0.5 * total_sq - 0.5 * width * total_live / tau) / (all_blocks * width)
    return (grad_obs, grad_tau)


def solution(mesh):
    in_specs = (
        P(("region", "block"), None, None),
        P(("region", "block"), None, None, None),
        P(("region", "block"), None, None),
        P(),
        P(("region", "block"), None),
        P(("region", "block"), None),
        P(("region", "block")),
    )
    out_specs = (P(("region", "block"), None, None), P())
    return jax.shard_map(shards, mesh=mesh, in_specs=in_specs, out_specs=out_specs, check_vma=False)
```

profile of v0, /device:TPU:0, one launch (start us, length us, event | category | flops | bytes accessed | tf_op | source)
XLA Modules:
  0.0 102.5 jit_solution(590737278167899570)
XLA Ops:
  7.2 0.0 copy-start
  7.2 0.0 copy-start.2
  7.2 0.0 copy-start.1
  7.2 0.0 all-gather.2.cloned.1.call-start
  7.2 0.7 all-gather.2.cloned.1.call-update
  7.9 0.2 copy-done.2
  8.1 4.8 %collective-permute-start = (bf16[16,32,128]{2,1,0:T(8,128)(2,1)S(1)}, bf16[16,32,128]{2,1,0:T(8,128)(2,1)S(1)}, u32[]{:S(2)}, u32[]{:S(2)}) collective-permute-start(bf16[16,32,128]{2,1,0:T(8,128)(2,1)S(1)} %copy-done.2), channel_id=1, source_target_pairs={{0,8},{8,16},{16,24},{1,9},{9,17},{17,25},{2,10},{10,18},{18,26},{... | collective-permute-start | bytes 393224 | tf_op jit(solution)/shard_map/ppermute | solution.py:10
  13.0 0.7 fusion.33
  13.8 0.8 select_reduce_fusion.1
  14.6 0.8 slice_bitcast_fusion.1
  15.4 0.1 convert_reduce_fusion
  15.5 0.7 add.50
  16.1 4.9 %all-to-all-start = ((s32[8,1,4]{2,1,0:T(1,128)}), s32[8,1,4]{2,1,0:T(1,128)S(1)}, u32[]{:S(2)}, u32[]{:S(2)}) async-start(s32[8,1,4]{2,1,0:T(1,128)} %bitcast.11), calls=%async_computation | async-start | bytes 8192 | tf_op jit(solution)/shard_map/all_to_all | solution.py:55
  21.7 0.8 and_bitcast_fusion.1
  22.4 0.7 broadcast_multiply_fusion
  23.2 0.0 collective-permute-done
  23.2 0.6 gather_fusion.1
  23.8 10.7 %all-gather.2.cloned.1.call-done = bf16[128,32,128]{2,1,0:T(8,128)(2,1)} async-done(((bf16[16,32,128]{2,1,0:T(8,128)(2,1)}), bf16[128,32,128]{2,1,0:T(8,128)(2,1)}) %all-gather.2.cloned.1.call-update) | async-done | bytes 1048592 | tf_op jit(solution)/shard_map/all_gather | solution.py:31
  34.5 1.8 %gather_fusion = bf16[16,32,128]{2,1,0:T(8,128)(2,1)S(1)} fusion(bf16[128,32,128]{2,1,0:T(8,128)(2,1)} %all-gather.2.cloned.1.call-done, s32[1024]{0:T(1024)S(1)} %pad_clamp_fusion.1), kind=kCustom, calls=%fused_computation | custom fusion | bytes 262208 | tf_op jit(solution)/shard_map/jit(_take)/gather | solution.py:32
  36.3 1.4 %convolution_subtract_fusion.1 = f32[16,32,128]{2,1,0:T(8,128)S(1)} fusion(bf16[16,2,128,128]{3,2,1,0:T(8,128)(2,1)} %param.8, bf16[16,32,128]{2,1,0:T(8,128)(2,1)S(1)} %copy-done.2, bf16[16,32,128]{2,1,0:T(8,128)(2,1)S(1)} %gather_fusion, pred[16]{0:T(512)(128)(4,1)S(1)} %get-tuple-element.6), kind=kOutput, calls=%fused_computation.5 | convolution fusion | flops 16973824 | bytes 1048592 | tf_op jit(solution)/shard_map/bcj,bjk->bck/dot_general | solution.py:37
  37.6 0.0 copy-done
  37.6 0.0 copy-done.1
  37.7 0.6 fusion.12
  38.2 0.4 fusion.18
  38.6 0.4 convolution_negate_fusion.1
  39.0 0.7 fusion.16
  39.8 0.9 copy.17
  40.7 0.0 all-to-all-done
  40.7 3.5 %all-to-all-start.1 = ((f32[8,4,32,128]{3,1,2,0:T(4,128)}), f32[8,4,32,128]{3,1,2,0:T(4,128)S(1)}, u32[]{:S(2)}, u32[]{:S(2)}) async-start(f32[8,4,32,128]{3,1,2,0:T(4,128)} %copy.17), calls=%async_computation.1 | async-start | bytes 1048576 | tf_op jit(solution)/shard_map/all_to_all | solution.py:54
  44.2 0.6 fusion.47
  44.8 0.5 broadcast.119
  45.3 0.7 reduce.3
  46.0 0.1 eq.68
  46.0 0.4 convolution_negate_fusion
  46.4 0.4 fusion.13
  46.8 0.1 copy.21
  46.9 1.3 %collective-permute-start.1 = (f32[16,32,128]{2,1,0:T(8,128)S(1)}, f32[16,32,128]{2,1,0:T(8,128)S(1)}, u32[]{:S(2)}, u32[]{:S(2)}) collective-permute-start(f32[16,32,128]{2,1,0:T(8,128)S(1)} %copy.21), channel_id=1, source_target_pairs={{8,0},{16,8},{24,16},{9,1},{17,9},{25,17},{10,2},{18,10},{26,18},{... | collective-permute-start | bytes 786440 | tf_op jit(solution)/shard_map/ppermute | solution.py:10
  48.2 44.3 %all-reduce = (f32[32]{0:T(128)S(1)}, f32[]{:T(128)}) all-reduce(f32[32]{0:T(128)S(1)} %get-tuple-element.12, f32[]{:T(128)} %fusion.47), channel_id=1, replica_groups=mesh['region'=4,'block'=8] {'region','block'}, use_global_device_ids=true, to_apply=%region_5.6 | all-reduce | flops 33 | bytes 264 | tf_op jit(solution)/shard_map/psum | solution.py:72
  93.1 0.0 copy-start.3
  93.2 0.6 copy-done.3
  93.8 0.5 fusion.43
  94.3 0.0 all-to-all-done.1
  94.3 0.1 copy.18
  94.5 0.3 fusion.35
  94.8 0.0 collective-permute-done.1
  94.8 0.9 fusion.15
  (5 shorter events, 0.1 us)
Async XLA Ops:
  7.2 30.5 %copy-start = (bf16[16,128,128]{2,1,0:T(8,128)(2,1)S(1)}, bf16[16,128,128]{2,1,0:T(8,128)(2,1)}, u32[]{:S(2)}) copy-start(bf16[16,128,128]{2,1,0:T(8,128)(2,1)} %param.9) | copy-start | bytes 1572868
  7.2 1.0 copy-start.2
  7.2 30.5 %copy-start.1 = (bf16[16,2,128,128]{3,2,1,0:T(8,128)(2,1)S(1)}, bf16[16,2,128,128]{3,2,1,0:T(8,128)(2,1)}, u32[]{:S(2)}) copy-start(bf16[16,2,128,128]{3,2,1,0:T(8,128)(2,1)} %param.8) | copy-start | bytes 3145732
  7.2 27.3 %all-gather.2.cloned.1.call-start = ((), (), s32[]{:S(2)}) async-start(), calls=%async_computation.2 | async-start | bytes 1179648 | tf_op jit(solution)/shard_map/all_gather | solution.py:31
  8.1 15.0 %collective-permute-start = (bf16[16,32,128]{2,1,0:T(8,128)(2,1)S(1)}, bf16[16,32,128]{2,1,0:T(8,128)(2,1)S(1)}, u32[]{:S(2)}, u32[]{:S(2)}) collective-permute-start(bf16[16,32,128]{2,1,0:T(8,128)(2,1)S(1)} %copy-done.2), channel_id=1, source_target_pairs={{0,8},{8,16},{16,24},{1,9},{9,17},{17,25},{2,10},{10,18},{18,26},{... | collective-permute-start | bytes 393224 | tf_op jit(solution)/shard_map/ppermute | solution.py:10
  16.1 24.5 %all-to-all-start = ((s32[8,1,4]{2,1,0:T(1,128)}), s32[8,1,4]{2,1,0:T(1,128)S(1)}, u32[]{:S(2)}, u32[]{:S(2)}) async-start(s32[8,1,4]{2,1,0:T(1,128)} %bitcast.11), calls=%async_computation | async-start | bytes 8192 | tf_op jit(solution)/shard_map/all_to_all | solution.py:55
  40.7 53.7 %all-to-all-start.1 = ((f32[8,4,32,128]{3,1,2,0:T(4,128)}), f32[8,4,32,128]{3,1,2,0:T(4,128)S(1)}, u32[]{:S(2)}, u32[]{:S(2)}) async-start(f32[8,4,32,128]{3,1,2,0:T(4,128)} %copy.17), calls=%async_computation.1 | async-start | bytes 1048576 | tf_op jit(solution)/shard_map/all_to_all | solution.py:54
  46.9 47.9 %collective-permute-start.1 = (f32[16,32,128]{2,1,0:T(8,128)S(1)}, f32[16,32,128]{2,1,0:T(8,128)S(1)}, u32[]{:S(2)}, u32[]{:S(2)}) collective-permute-start(f32[16,32,128]{2,1,0:T(8,128)S(1)} %copy.21), channel_id=1, source_target_pairs={{8,0},{16,8},{24,16},{9,1},{17,9},{25,17},{10,2},{18,10},{26,18},{... | collective-permute-start | bytes 786440 | tf_op jit(solution)/shard_map/ppermute | solution.py:10
  93.1 0.7 copy-start.3
Sparse Core Ops, SparseCore 0:
  9.6 24.7 all-gather.1
where the time goes:
time: 103 us
  blocking collectives  44.3 us (43%)
  between operations  15.5 us (15%)
  starting transfers between devices  14.5 us (14%)
  waiting for transfers between devices  11.4 us (11%)
  other arithmetic  6.61 us (6%)
  local copies, waits for them, and re-layouts  5.62 us (5%)
  matrix products  4.57 us (4%)
    psum x1, blocking collectives, shards(): total_sq, total_live = lax.psum((squares, live_count), ('region', 'block'))  44.3 us
    all_gather x1, waiting for transfers between devices, shards(): region_all = lax.all_gather(obs, 'block', axis=0, tiled=True)  10.7 us
    ppermute x2, starting transfers between devices, passed_along(): lax.ppermute(value, axis, [(source, source + steps) for source in range(l...  6.13 us
    all_to_all x1, starting transfers between devices, shards(): lax.all_to_all(request, 'block', split_axis=0, concat_axis=0, tiled=True)  4.88 us
    all_to_all x1, starting transfers between devices, shards(): lax.all_to_all(placed, 'block', split_axis=0, concat_axis=0, tiled=True)  3.49 us
  transfers between devices with their start and end apart: 5, of which 1 were waited for; matrix products, arithmetic and copies ran while one was open for 15% of the time, Pallas kernels for 0%

commit v1 on v0

--- a/solution.py
+++ b/solution.py
@@ -2,6 +2,27 @@
 import jax.numpy as jnp
 from jax import lax
 from jax.sharding import PartitionSpec as P
+
+
+def do_the_levels_all(vector, pos_dim):
+    newest = list(vector.shape[1:])
+    newest[pos_dim] *= vector.shape[0]
+    shaped = jnp.moveaxis(vector, 0, pos_dim).reshape(newest)
+    return shaped
+
+
+def pass_plate_in(w_in, axis_tag, axis_no):
+    count_all = jax.lax.axis_size(axis_tag)
+    runs = []
+    for k0 in range(count_all):
+        runs.append((k0, (k0 + 1) % count_all))
+    buffers = [w_in]
+    while len(buffers) < count_all:
+        buffers.append(jax.lax.ppermute(buffers[-1], axis_tag, runs))
+    x_new = jax.lax.axis_index(axis_tag)
+    buffers = jnp.stack(buffers)[(x_new - jnp.arange(count_all)) % count_all]
+    piece_next = do_the_levels_all(buffers, axis_no)
+    return piece_next
 
 
 def passed_along(value, axis, steps):
@@ -28,7 +49,7 @@
     filled = jnp.sum(match, axis=0)
     req_flat = jnp.sum(match * slot_one[:, None], axis=0) + (1 - filled) * nbd
     request = req_flat.reshape(nblock, cap_size)
-    region_all = lax.all_gather(obs, "block", axis=0, tiled=True)
+    region_all = pass_plate_in(obs, "block", 0)
     near = jnp.take(region_all, dest * nbd + slot_one, axis=0)
     previous = passed_along(obs, "region", 1)
     far = jnp.take(previous, slot_two, axis=0)

time: 103 us -> 113 us (1.097)
  waiting for transfers between devices: 11.4 us -> 36 us
  between operations: 15.5 us -> 2.19 us
  other arithmetic: 6.61 us -> 3.16 us
  local copies, waits for them, and re-layouts: 5.62 us -> 8.64 us
    ppermute x0 -> x7, waiting for transfers between devices: none -> 35.9 us  [pass_plate_in(): buffers.append(jax.lax.ppermute(buffers[-1], axis_tag, runs))]
    all_gather x1 -> x0, waiting for transfers between devices: 10.7 us -> none  [shards(): region_all = lax.all_gather(obs, 'block', axis=0, tiled=True)]
    gather x0 -> x1, local copies, waits for them, and re-layouts: none -> 1.67 us  [pass_plate_in(): buffers = jnp.stack(buffers)[(x_new - jnp.arange(count_all)) % count_all]]
    unnamed x8 -> x19, local copies, waits for them, and re-layouts: 0.87 us -> 2.18 us
  transfers between devices with their start and end apart: 5 -> 11, of which waited for: 1 -> 6; matrix products, arithmetic and copies ran while one was open for 15% -> 12% of each run, Pallas kernels for 0% -> 0%
where the time goes in v1:
time: 113 us
  blocking collectives  44.3 us (39%)
  waiting for transfers between devices  36 us (32%)
  starting transfers between devices  15.3 us (14%)
  local copies, waits for them, and re-layouts  8.64 us (8%)
  matrix products  3.51 us (3%)
  other arithmetic  3.16 us (3%)
  between operations  2.19 us (2%)
    psum x1, blocking collectives, shards(): total_sq, total_live = lax.psum((squares, live_count), ('region', 'block'))  44.3 us
    ppermute x7, waiting for transfers between devices, pass_plate_in(): buffers.append(jax.lax.ppermute(buffers[-1], axis_tag, runs))  35.9 us
    ppermute x2, starting transfers between devices, passed_along(): lax.ppermute(value, axis, [(source, source + steps) for source in range(l...  5.84 us
    all_to_all x1, starting transfers between devices, shards(): lax.all_to_all(request, 'block', split_axis=0, concat_axis=0, tiled=True)  4.88 us
    all_to_all x1, starting transfers between devices, shards(): lax.all_to_all(placed, 'block', split_axis=0, concat_axis=0, tiled=True)  3.49 us
  transfers between devices with their start and end apart: 11, of which 6 were waited for; matrix products, arithmetic and copies ran while one was open for 12% of the time, Pallas kernels for 0%

profile of v1, /device:TPU:0, one launch (start us, length us, event | category | flops | bytes accessed | tf_op | source)
XLA Modules:
  0.0 113.0 jit_solution(10701072475782666037)
XLA Ops:
  0.6 0.0 copy-start
  0.7 0.5 collective-permute-start
  1.2 4.5 %collective-permute-start.7 = (bf16[16,32,128]{2,1,0:T(8,128)(2,1)}, bf16[16,32,128]{2,1,0:T(8,128)(2,1)S(1)}, u32[]{:S(2)}, u32[]{:S(2)}) collective-permute-start(bf16[16,32,128]{2,1,0:T(8,128)(2,1)} %param.7), channel_id=1, source_target_pairs={{0,8},{8,16},{16,24},{1,9},{9,17},{17,25},{2,10},{10,18},{18,26},{... | collective-permute-start | bytes 393224 | tf_op jit(solution)/shard_map/ppermute | solution.py:31
  5.7 0.1 fusion.33
  5.8 0.2 select_reduce_fusion.1
  6.0 0.5 copy-done.4
  6.5 0.1 convert_reduce_fusion
  6.6 0.7 add.75
  7.3 4.9 %all-to-all-start = ((s32[8,1,4]{2,1,0:T(1,128)}), s32[8,1,4]{2,1,0:T(1,128)S(1)}, u32[]{:S(2)}, u32[]{:S(2)}) async-start(s32[8,1,4]{2,1,0:T(1,128)} %bitcast.21), calls=%async_computation | async-start | bytes 8192 | tf_op jit(solution)/shard_map/all_to_all | solution.py:76
  12.2 0.9 bitcast_dynamic-update-slice_fusion.7
  13.8 0.0 copy-start.5
  13.8 0.6 copy-done.5
  14.4 0.1 broadcast_multiply_fusion
  14.5 0.0 collective-permute-done
  14.5 0.6 collective-permute-start.1
  15.1 0.0 collective-permute-done.7
  15.1 0.6 gather_fusion.2
  15.7 5.1 %collective-permute-done.1 = bf16[16,32,128]{2,1,0:T(8,128)(2,1)S(1)} collective-permute-done((bf16[16,32,128]{2,1,0:T(8,128)(2,1)S(1)}, bf16[16,32,128]{2,1,0:T(8,128)(2,1)S(1)}, u32[]{:S(2)}, u32[]{:S(2)}) %collective-permute-start.1) | collective-permute-done | bytes 131104 | tf_op jit(solution)/shard_map/ppermute | solution.py:21
  20.8 0.0 collective-permute-start.2
  20.9 6.2 %collective-permute-done.2 = bf16[16,32,128]{2,1,0:T(8,128)(2,1)S(1)} collective-permute-done((bf16[16,32,128]{2,1,0:T(8,128)(2,1)S(1)}, bf16[16,32,128]{2,1,0:T(8,128)(2,1)S(1)}, u32[]{:S(2)}, u32[]{:S(2)}) %collective-permute-start.2) | collective-permute-done | bytes 131104 | tf_op jit(solution)/shard_map/ppermute | solution.py:21
  27.0 0.0 collective-permute-start.3
  27.0 6.2 %collective-permute-done.3 = bf16[16,32,128]{2,1,0:T(8,128)(2,1)S(1)} collective-permute-done((bf16[16,32,128]{2,1,0:T(8,128)(2,1)S(1)}, bf16[16,32,128]{2,1,0:T(8,128)(2,1)S(1)}, u32[]{:S(2)}, u32[]{:S(2)}) %collective-permute-start.3) | collective-permute-done | bytes 131104 | tf_op jit(solution)/shard_map/ppermute | solution.py:21
  33.2 6.2 %collective-permute-done.4 = bf16[16,32,128]{2,1,0:T(8,128)(2,1)S(1)} collective-permute-done((bf16[16,32,128]{2,1,0:T(8,128)(2,1)S(1)}, bf16[16,32,128]{2,1,0:T(8,128)(2,1)S(1)}, u32[]{:S(2)}, u32[]{:S(2)}) %collective-permute-start.4) | collective-permute-done | bytes 131104 | tf_op jit(solution)/shard_map/ppermute | solution.py:21
  39.4 6.2 %collective-permute-done.5 = bf16[16,32,128]{2,1,0:T(8,128)(2,1)S(1)} collective-permute-done((bf16[16,32,128]{2,1,0:T(8,128)(2,1)S(1)}, bf16[16,32,128]{2,1,0:T(8,128)(2,1)S(1)}, u32[]{:S(2)}, u32[]{:S(2)}) %collective-permute-start.5) | collective-permute-done | bytes 131104 | tf_op jit(solution)/shard_map/ppermute | solution.py:21
  45.6 6.2 %collective-permute-done.6 = bf16[16,32,128]{2,1,0:T(8,128)(2,1)S(1)} collective-permute-done((bf16[16,32,128]{2,1,0:T(8,128)(2,1)S(1)}, bf16[16,32,128]{2,1,0:T(8,128)(2,1)S(1)}, u32[]{:S(2)}, u32[]{:S(2)}) %collective-permute-start.6) | collective-permute-done | bytes 131104 | tf_op jit(solution)/shard_map/ppermute | solution.py:21
  51.8 0.0 copy-start.1
  51.8 1.7 %gather_fusion = bf16[8,16,32,128]{3,2,1,0:T(8,128)(2,1)} fusion(bf16[8,16,32,128]{3,2,1,0:T(8,128)(2,1)S(1)} %bitcast_dynamic-update-slice_fusion, s32[1024]{0:T(1024)S(1)} %pad_clamp_fusion.2), kind=kCustom, calls=%fused_computation | custom fusion | bytes 2097184 | tf_op jit(solution)/shard_map/gather | solution.py:23
  53.5 1.8 %gather_fusion.1 = bf16[16,32,128]{2,1,0:T(8,128)(2,1)S(1)} fusion(bf16[128,32,128]{2,1,0:T(8,128)(2,1)} %bitcast.74, s32[1024]{0:T(1024)S(1)} %pad_clamp_fusion.1), kind=kCustom, calls=%fused_computation.1 | custom fusion | bytes 262208 | tf_op jit(solution)/shard_map/jit(_take)/gather | solution.py:53
  55.3 0.3 convolution_subtract_fusion.1
  55.7 0.6 fusion.12
  56.2 0.4 fusion.18
  56.6 0.4 convolution_negate_fusion.1
  57.0 0.7 fusion.16
  57.8 0.9 copy.17
  58.7 3.5 %all-to-all-start.1 = ((f32[8,4,32,128]{3,1,2,0:T(4,128)}), f32[8,4,32,128]{3,1,2,0:T(4,128)S(1)}, u32[]{:S(2)}, u32[]{:S(2)}) async-start(f32[8,4,32,128]{3,1,2,0:T(4,128)} %copy.17), calls=%async_computation.1 | async-start | bytes 1048576 | tf_op jit(solution)/shard_map/all_to_all | solution.py:75
  62.2 0.6 fusion.49
  62.8 0.5 broadcast.188
  63.3 0.7 reduce.3
  63.9 0.1 eq.70
  64.0 0.4 convolution_negate_fusion
  64.4 0.4 fusion.13
  64.8 0.1 copy.21
  64.9 1.3 %collective-permute-start.8 = (f32[16,32,128]{2,1,0:T(8,128)S(1)}, f32[16,32,128]{2,1,0:T(8,128)S(1)}, u32[]{:S(2)}, u32[]{:S(2)}) collective-permute-start(f32[16,32,128]{2,1,0:T(8,128)S(1)} %copy.21), channel_id=1, source_target_pairs={{8,0},{16,8},{24,16},{9,1},{17,9},{25,17},{10,2},{18,10},{26,18},{... | collective-permute-start | bytes 786440 | tf_op jit(solution)/shard_map/ppermute | solution.py:31
  66.2 44.3 %all-reduce = (f32[32]{0:T(128)S(1)}, f32[]{:T(128)}) all-reduce(f32[32]{0:T(128)S(1)} %get-tuple-element.12, f32[]{:T(128)} %fusion.49), channel_id=1, replica_groups=mesh['region'=4,'block'=8] {'region','block'}, use_global_device_ids=true, to_apply=%region_5.6 | all-reduce | flops 33 | bytes 264 | tf_op jit(solution)/shard_map/psum | solution.py:93
  111.2 0.5 fusion.45
  111.7 0.1 copy.18
  111.8 0.3 fusion.35
  112.2 0.9 fusion.15
  (29 shorter events, 0.3 us)
Async XLA Ops:
  0.6 55.0 %copy-start = (bf16[16,128,128]{2,1,0:T(8,128)(2,1)S(1)}, bf16[16,128,128]{2,1,0:T(8,128)(2,1)}, u32[]{:S(2)}) copy-start(bf16[16,128,128]{2,1,0:T(8,128)(2,1)} %param.9) | copy-start | bytes 1572868
  0.6 5.1 %copy-start.3 = (s32[16,1]{0,1:T(1,128)S(1)}, s32[16,1]{0,1:T(1,128)}, u32[]{:S(2)}) copy-start(s32[16,1]{0,1:T(1,128)} %param.11) | copy-start | bytes 196
  0.7 13.9 %collective-permute-start = (bf16[16,32,128]{2,1,0:T(8,128)(2,1)}, bf16[16,32,128]{2,1,0:T(8,128)(2,1)S(1)}, u32[]{:S(2)}, u32[]{:S(2)}) collective-permute-start(bf16[16,32,128]{2,1,0:T(8,128)(2,1)} %param.7), channel_id=1, source_target_pairs={{0,1},{1,2},{2,3},{3,4},{4,5},{5,6},{6,7},{7,0},{8,9},{9,10},{10,1... | collective-permute-start | bytes 393224 | tf_op jit(solution)/shard_map/ppermute | solution.py:21
  1.2 13.9 %collective-permute-start.7 = (bf16[16,32,128]{2,1,0:T(8,128)(2,1)}, bf16[16,32,128]{2,1,0:T(8,128)(2,1)S(1)}, u32[]{:S(2)}, u32[]{:S(2)}) collective-permute-start(bf16[16,32,128]{2,1,0:T(8,128)(2,1)} %param.7), channel_id=1, source_target_pairs={{0,8},{8,16},{16,24},{1,9},{9,17},{17,25},{2,10},{10,18},{18,26},{... | collective-permute-start | bytes 393224 | tf_op jit(solution)/shard_map/ppermute | solution.py:31
  5.8 0.7 copy-start.4
  7.3 51.4 %all-to-all-start = ((s32[8,1,4]{2,1,0:T(1,128)}), s32[8,1,4]{2,1,0:T(1,128)S(1)}, u32[]{:S(2)}, u32[]{:S(2)}) async-start(s32[8,1,4]{2,1,0:T(1,128)} %bitcast.21), calls=%async_computation | async-start | bytes 8192 | tf_op jit(solution)/shard_map/all_to_all | solution.py:76
  13.8 0.7 copy-start.5
  14.5 6.3 %collective-permute-start.1 = (bf16[16,32,128]{2,1,0:T(8,128)(2,1)S(1)}, bf16[16,32,128]{2,1,0:T(8,128)(2,1)S(1)}, u32[]{:S(2)}, u32[]{:S(2)}) collective-permute-start(bf16[16,32,128]{2,1,0:T(8,128)(2,1)S(1)} %collective-permute-done), channel_id=1, source_target_pairs={{0,1},{1,2},{2,3},{3,4},{4,5},{5,6},{6,7},{7,0},{8,9},{9,10},{10,1... | collective-permute-start | bytes 393224 | tf_op jit(solution)/shard_map/ppermute | solution.py:21
  20.8 6.2 %collective-permute-start.2 = (bf16[16,32,128]{2,1,0:T(8,128)(2,1)S(1)}, bf16[16,32,128]{2,1,0:T(8,128)(2,1)S(1)}, u32[]{:S(2)}, u32[]{:S(2)}) collective-permute-start(bf16[16,32,128]{2,1,0:T(8,128)(2,1)S(1)} %collective-permute-done.1), channel_id=1, source_target_pairs={{0,1},{1,2},{2,3},{3,4},{4,5},{5,6},{6,7},{7,0},{8,9},{9,10},{10,1... | collective-permute-start | bytes 393224 | tf_op jit(solution)/shard_map/ppermute | solution.py:21
  27.0 6.2 %collective-permute-start.3 = (bf16[16,32,128]{2,1,0:T(8,128)(2,1)S(1)}, bf16[16,32,128]{2,1,0:T(8,128)(2,1)S(1)}, u32[]{:S(2)}, u32[]{:S(2)}) collective-permute-start(bf16[16,32,128]{2,1,0:T(8,128)(2,1)S(1)} %collective-permute-done.2), channel_id=1, source_target_pairs={{0,1},{1,2},{2,3},{3,4},{4,5},{5,6},{6,7},{7,0},{8,9},{9,10},{10,1... | collective-permute-start | bytes 393224 | tf_op jit(solution)/shard_map/ppermute | solution.py:21
  33.2 6.2 %collective-permute-start.4 = (bf16[16,32,128]{2,1,0:T(8,128)(2,1)S(1)}, bf16[16,32,128]{2,1,0:T(8,128)(2,1)S(1)}, u32[]{:S(2)}, u32[]{:S(2)}) collective-permute-start(bf16[16,32,128]{2,1,0:T(8,128)(2,1)S(1)} %collective-permute-done.3), channel_id=1, source_target_pairs={{0,1},{1,2},{2,3},{3,4},{4,5},{5,6},{6,7},{7,0},{8,9},{9,10},{10,1... | collective-permute-start | bytes 393224 | tf_op jit(solution)/shard_map/ppermute | solution.py:21
  39.4 6.2 %collective-permute-start.5 = (bf16[16,32,128]{2,1,0:T(8,128)(2,1)S(1)}, bf16[16,32,128]{2,1,0:T(8,128)(2,1)S(1)}, u32[]{:S(2)}, u32[]{:S(2)}) collective-permute-start(bf16[16,32,128]{2,1,0:T(8,128)(2,1)S(1)} %collective-permute-done.4), channel_id=1, source_target_pairs={{0,1},{1,2},{2,3},{3,4},{4,5},{5,6},{6,7},{7,0},{8,9},{9,10},{10,1... | collective-permute-start | bytes 393224 | tf_op jit(solution)/shard_map/ppermute | solution.py:21
  45.6 6.2 %collective-permute-start.6 = (bf16[16,32,128]{2,1,0:T(8,128)(2,1)S(1)}, bf16[16,32,128]{2,1,0:T(8,128)(2,1)S(1)}, u32[]{:S(2)}, u32[]{:S(2)}) collective-permute-start(bf16[16,32,128]{2,1,0:T(8,128)(2,1)S(1)} %collective-permute-done.5), channel_id=1, source_target_pairs={{0,1},{1,2},{2,3},{3,4},{4,5},{5,6},{6,7},{7,0},{8,9},{9,10},{10,1... | collective-permute-start | bytes 393224 | tf_op jit(solution)/shard_map/ppermute | solution.py:21
  51.8 3.5 %copy-start.1 = (bf16[16,2,128,128]{3,2,1,0:T(8,128)(2,1)S(1)}, bf16[16,2,128,128]{3,2,1,0:T(8,128)(2,1)}, u32[]{:S(2)}) copy-start(bf16[16,2,128,128]{3,2,1,0:T(8,128)(2,1)} %param.8) | copy-start | bytes 3145732
  53.5 1.9 %copy-start.2 = (bf16[16,32,128]{2,1,0:T(8,128)(2,1)S(1)}, bf16[16,32,128]{2,1,0:T(8,128)(2,1)}, u32[]{:S(2)}) copy-start(bf16[16,32,128]{2,1,0:T(8,128)(2,1)} %param.7) | copy-start | bytes 393220
  58.7 53.0 %all-to-all-start.1 = ((f32[8,4,32,128]{3,1,2,0:T(4,128)}), f32[8,4,32,128]{3,1,2,0:T(4,128)S(1)}, u32[]{:S(2)}, u32[]{:S(2)}) async-start(f32[8,4,32,128]{3,1,2,0:T(4,128)} %copy.17), calls=%async_computation.1 | async-start | bytes 1048576 | tf_op jit(solution)/shard_map/all_to_all | solution.py:75
  64.9 47.2 %collective-permute-start.8 = (f32[16,32,128]{2,1,0:T(8,128)S(1)}, f32[16,32,128]{2,1,0:T(8,128)S(1)}, u32[]{:S(2)}, u32[]{:S(2)}) collective-permute-start(f32[16,32,128]{2,1,0:T(8,128)S(1)} %copy.21), channel_id=1, source_target_pairs={{8,0},{16,8},{24,16},{9,1},{17,9},{25,17},{10,2},{18,10},{26,18},{... | collective-permute-start | bytes 786440 | tf_op jit(solution)/shard_map/ppermute | solution.py:31
